TPU v7x, 32 devices: a whole 2x2x4 slice. The times are simulated.
32 devices in a mesh: gz: 4 (over z), lat: 8 (over y, x, core).
Axes of the slice: x: 2, y: 2, z: 4, core: 2. Of those that a mesh axis runs over, the one named last changes fastest.
Arguments:
- features: bfloat16 [8, 512, 1536], P('lat', 'gz'), may hold values from -6 to 6
- input_map: bfloat16 [8, 512, 128], P('lat', 'gz'), may hold values from -0.5 to 0.5
- output_map: bfloat16 [8, 512, 128], P('lat', 'gz'), may hold values from -0.5 to 0.5
- step_size: float32 [8, 512, 24], P('lat', 'gz'), may hold values from 0.008 to 0.11, as said below
- decay_rate: float32 [24], replicated, may hold values from 0.005859375 to 1, as said below
- skip_gain: float32 [24], replicated, may hold values from 0.5 to 1.5
- kernel: float32 [3, 1536], replicated, may hold values from -2.5 to 2.5
- cotangent: bfloat16 [8, 512, 1536], P(None, ('gz', 'lat')), may hold values from -23 to 23
Outputs:
- lateral_out: bfloat16 [8, 512, 1536], P(None, ('gz', 'lat'))
- grad_features: bfloat16 [8, 512, 1536], P('lat', 'gz')
- grad_input_map: bfloat16 [8, 512, 128], P('lat', 'gz')
- grad_output_map: bfloat16 [8, 512, 128], P('lat', 'gz')
- grad_kernel: float32 [3, 1536], replicated
Inputs may be any that keep to these rules, and one draw needn't show every extreme that they name: `step_size`: positive step sizes. `decay_rate`: positive rates.
All inputs are finite; a program needn't handle non-finite values.
Results may differ from a plain program's by a relative error of at most 0.0069.
Values may be sent and summed in bfloat16 or wider, within the bound.
A program may use at most 128 MiB of HBM per device.

v0:
```python
import math
import jax
import jax.numpy as jnp
from jax import lax
from jax.sharding import PartitionSpec as P


def prefix(part, axis, combine, identity, reverse):
    count = lax.axis_size(axis)
    place = lax.axis_index(axis)
    ahead = count - 1 - place if reverse else place
    gathered = jax.tree.map(lambda a: lax.all_gather(a, axis), part)
    state = jax.tree.map(lambda a, e: jnp.zeros_like(a) + jnp.asarray(e, a.dtype), part, identity)

    def one(step, state):
        source = count - 1 - step if reverse else step
        return combine(
            state, jax.tree.map(lambda a: lax.dynamic_index_in_dim(a, source, 0, False), gathered)
        )

    return lax.fori_loop(0, ahead, one, state)


def decay_head(log_decay, step_head):
    length = log_decay.shape[0]
    row_index = lax.broadcasted_iota(jnp.int32, (length, length), 0)
    col_index = lax.broadcasted_iota(jnp.int32, (length, length), 1)
    spread = log_decay[:, None] - log_decay[None, :]
    return jnp.exp(jnp.where(row_index >= col_index, spread, -jnp.inf)) * step_head[None, :]


def local_terms(input_block, output_block, step_block, decay_rate):
    log_decay = jnp.cumsum(-step_block * decay_rate[None, :], axis=0)
    block_total = log_decay[-1]
    out_weight = step_block * jnp.exp(block_total[None, :] - log_decay)
    map_product = jnp.dot(output_block, input_block.T, preferred_element_type=jnp.float32)
    decay_mask = jax.vmap(decay_head, in_axes=(1, 1))(log_decay, step_block)
    mix_weights = (map_product[None] * decay_mask).astype(jnp.bfloat16)
    in_weights = (input_block.astype(jnp.float32)[:, None, :] * out_weight[:, :, None]).astype(
        jnp.bfloat16
    )
    out_read = (
        output_block.astype(jnp.float32)[:, None, :] * jnp.exp(log_decay)[:, :, None]
    ).astype(jnp.bfloat16)
    return (log_decay, block_total, out_weight, mix_weights, in_weights, out_read)


def chain_combine(earlier, later):
    return (earlier[0] * later[0], later[0][:, :, None, None] * earlier[1] + later[1])


def head_pairs(heads_grad, heads_in, log_decay, step_block):
    length = heads_grad.shape[0]

    def accumulate(summed, pieces):
        grad_head, feat_head, head_log, step_head = pieces
        head_inner = jnp.dot(grad_head, feat_head.T, preferred_element_type=jnp.float32)
        return (summed + head_inner * decay_head(head_log, step_head), None)

    summed, unused = lax.scan(
        accumulate,
        jnp.zeros((length, length), jnp.float32),
        (jnp.swapaxes(heads_grad, 0, 1), jnp.swapaxes(heads_in, 0, 1), log_decay.T, step_block.T),
    )
    return summed.astype(jnp.bfloat16)


def lateral_sum(padded, kernel, extent, flip):
    tap_count = kernel.shape[0]
    summed = 0.0
    for tap_index in range(tap_count):
        anchor = tap_count - 1 - tap_index if flip else tap_index
        summed = summed + kernel[tap_index][None, None, :] * padded[anchor : anchor + extent]
    return summed


def kernel_terms(cotangent, padded, extent):
    tap_count = padded.shape[0] - extent + 1
    return jnp.stack(
        [
            jnp.einsum(
                "xzc,xzc->c",
                cotangent,
                padded[tap_index : tap_index + extent],
                preferred_element_type=jnp.float32,
            )
            for tap_index in range(tap_count)
        ]
    )


def per_device(
    features, input_map, output_map, step_size, decay_rate, skip_gain, kernel, cotangent
):
    columns, sections, channels = features.shape
    head_count = step_size.shape[2]
    head_size = channels // head_count
    state_size = input_map.shape[2]
    log_decay, block_total, out_weight, mix_weights, in_weights, out_read = jax.vmap(
        local_terms, in_axes=(0, 0, 0, None)
    )(input_map, output_map, step_size, decay_rate)
    heads_in = features.reshape(columns, sections, head_count, head_size)
    block_state = jnp.einsum(
        "cihp,cihn->chpn", heads_in, in_weights, preferred_element_type=jnp.float32
    )
    decay_step = jnp.exp(block_total)
    identity = (jnp.ones_like(decay_step), jnp.zeros_like(block_state))
    incoming = prefix((decay_step, block_state), "gz", chain_combine, identity, False)
    state_low = incoming[1].astype(jnp.bfloat16)
    within = jnp.einsum(
        "chji,cihp->cjhp", mix_weights, heads_in, preferred_element_type=jnp.float32
    )
    carried = jnp.einsum("cjhn,chpn->cjhp", out_read, state_low, preferred_element_type=jnp.float32)
    ssd_out = (
        (within + carried + skip_gain[None, None, :, None] * heads_in)
        .reshape(columns, sections, channels)
        .astype(jnp.bfloat16)
    )
    margin = kernel.shape[0] // 2
    row_total = columns * sections * lax.axis_size("gz") * lax.axis_size("lat")
    plane_out = lax.all_to_all(ssd_out, "lat", split_axis=1, concat_axis=0, tiled=True)
    extent = plane_out.shape[0]
    widths = ((margin, margin), (0, 0), (0, 0))
    padded_out = jnp.pad(plane_out, widths)
    lateral_out = lateral_sum(padded_out, kernel, extent, False).astype(jnp.bfloat16)
    grad_planes = lateral_sum(jnp.pad(cotangent, widths), kernel, extent, True).astype(jnp.bfloat16)
    grad_ssd = lax.all_to_all(grad_planes, "lat", split_axis=0, concat_axis=1, tiled=True)
    kernel_part = kernel_terms(cotangent, padded_out, extent)
    grad_kernel = lax.psum(kernel_part, ("gz", "lat")) / math.sqrt(row_total)
    heads_grad = grad_ssd.reshape(columns, sections, head_count, head_size)
    block_adjoint = jnp.einsum(
        "cjhn,cjhp->chpn", out_read, heads_grad, preferred_element_type=jnp.float32
    )
    outgoing = prefix((decay_step, block_adjoint), "gz", chain_combine, identity, True)
    adjoint_low = outgoing[1].astype(jnp.bfloat16)
    grad_features = jnp.einsum(
        "chji,cjhp->cihp", mix_weights, heads_grad, preferred_element_type=jnp.float32
    )
    grad_features = grad_features + jnp.einsum(
        "cihn,chpn->cihp", in_weights, adjoint_low, preferred_element_type=jnp.float32
    )
    grad_features = (
        (grad_features + skip_gain[None, None, :, None] * heads_grad)
        .reshape(columns, sections, channels)
        .astype(jnp.bfloat16)
    )
    pair_weights = jax.vmap(head_pairs)(heads_grad, heads_in, log_decay, step_size)
    grad_read = (
        (heads_grad * jnp.exp(log_decay)[..., None])
        .astype(jnp.bfloat16)
        .reshape(columns, sections, channels)
    )
    feat_weights = (
        (heads_in * out_weight[..., None]).astype(jnp.bfloat16).reshape(columns, sections, channels)
    )
    state_rows = state_low.reshape(columns, channels, state_size)
    adjoint_rows = adjoint_low.reshape(columns, channels, state_size)
    grad_output_map = jnp.einsum(
        "cji,cin->cjn", pair_weights, input_map, preferred_element_type=jnp.float32
    )
    grad_output_map = (
        grad_output_map
        + jnp.einsum("cjk,ckn->cjn", grad_read, state_rows, preferred_element_type=jnp.float32)
    ).astype(jnp.bfloat16)
    grad_input_map = jnp.einsum(
        "cji,cjn->cin", pair_weights, output_map, preferred_element_type=jnp.float32
    )
    grad_input_map = (
        grad_input_map
        + jnp.einsum("cik,ckn->cin", feat_weights, adjoint_rows, preferred_element_type=jnp.float32)
    ).astype(jnp.bfloat16)
    return (lateral_out, grad_features, grad_input_map, grad_output_map, grad_kernel)


def solution(mesh):
    in_specs = (
        P("lat", "gz", None),
        P("lat", "gz", None),
        P("lat", "gz", None),
        P("lat", "gz", None),
        P(),
        P(),
        P(),
        P(None, ("gz", "lat"), None),
    )
    out_specs = (
        P(None, ("gz", "lat"), None),
        P("lat", "gz", None),
        P("lat", "gz", None),
        P("lat", "gz", None),
        P(),
    )
    return jax.shard_map(
        per_device, mesh=mesh, in_specs=in_specs, out_specs=out_specs, check_vma=False
    )
```

profile of v0, /device:TPU:0, one launch (start us, length us, event | category | flops | bytes accessed | tf_op | source)
XLA Modules:
  0.0 232.7 jit_solution(5359161026547841634)
XLA Ops:
  7.2 0.8 copy.102
  8.0 0.8 negate_multiply_fusion
  9.2 1.2 copy.101
  10.4 0.8 bitcast_convert_fusion
  11.2 1.6 convolution_bitcast_fusion
  12.9 12.6 %all_gather.18 = f32[4,1,24]{2,1,0:T(1,128)S(1)} all-gather(f32[1,1,24]{2,1,0:T(1,128)S(1)} %get-tuple-element.337), channel_id=1, replica_groups=mesh['gz'=4,'lat'=8] {'gz'}, dimensions={0}, use_global_device_ids=true | all-gather | bytes 480 | tf_op jit(solution)/shard_map/all_gather | solution.py:12
  25.7 53.4 %all-gather.5.cloned.1.call-done = f32[96,64,128]{2,1,0:T(8,128)} async-done(((f32[24,64,128]{2,1,0:T(8,128)}), f32[96,64,128]{2,1,0:T(8,128)}) %all-gather.5.cloned.1.call-update) | async-done | bytes 3145744 | tf_op jit(solution)/shard_map/all_gather | solution.py:12
  79.3 0.7 fusion.21
  80.0 0.8 fusion.15
  80.8 0.7 copy.107
  81.5 0.5 broadcast.126
  82.1 3.0 %reduce.12 = bf16[128,1536]{1,0:T(8,128)(2,1)S(1)} reduce(bf16[128,1,1536]{2,1,0:T(2,128)(2,1)S(1)} %bitcast.167, bf16[]{:T(256)} %broadcast.126), dimensions={1}, to_apply=%bitcast.130.reduce_sub_computation | reduce | bytes 786434
  85.1 1.0 reshape.339
  86.1 3.7 %all-to-all-start = ((bf16[8,2,12288]{2,1,0:T(2,128)(2,1)}), bf16[8,2,12288]{2,1,0:T(2,128)(2,1)S(1)}, u32[]{:S(2)}, u32[]{:S(2)}) async-start(bf16[8,2,12288]{2,1,0:T(2,128)(2,1)} %reshape.339), calls=%async_computation | async-start | bytes 786432 | tf_op jit(solution)/shard_map/all_to_all | solution.py:121
  90.0 8.1 %all-to-all-done = bf16[8,2,12288]{2,1,0:T(2,128)(2,1)S(1)} async-done(((bf16[8,2,12288]{2,1,0:T(2,128)(2,1)}), bf16[8,2,12288]{2,1,0:T(2,128)(2,1)S(1)}, u32[]{:S(2)}, u32[]{:S(2)}) %all-to-all-start) | async-done | bytes 393248 | tf_op jit(solution)/shard_map/all_to_all | solution.py:121
  98.0 0.4 reshape.340
  98.9 40.9 %psum.7 = f32[3,1536]{1,0:T(4,128)S(1)} all-reduce(f32[3,1536]{1,0:T(4,128)S(1)} %pad_maximum_fusion), channel_id=1, replica_groups=mesh['gz'=4,'lat'=8] {'gz','lat'}, use_global_device_ids=true, to_apply=%region_7.8 | all-reduce | flops 4608 | bytes 36864 | tf_op jit(solution)/shard_map/psum | solution.py:129
  139.7 1.2 add_convert_fusion
  140.9 3.6 %all-to-all-start.1 = ((bf16[8,16,1536]{2,1,0:T(8,128)(2,1)}), bf16[8,16,1536]{2,1,0:T(8,128)(2,1)S(1)}, u32[]{:S(2)}, u32[]{:S(2)}) async-start(bf16[8,16,1536]{2,1,0:T(8,128)(2,1)} %get-tuple-element.338), calls=%async_computation.1 | async-start | bytes 786432 | tf_op jit(solution)/shard_map/all_to_all | solution.py:127
  144.7 0.6 broadcast_multiply_fusion
  145.4 7.5 %all-to-all-done.1 = bf16[8,16,1536]{2,1,0:T(8,128)(2,1)S(1)} async-done(((bf16[8,16,1536]{2,1,0:T(8,128)(2,1)}), bf16[8,16,1536]{2,1,0:T(8,128)(2,1)S(1)}, u32[]{:S(2)}, u32[]{:S(2)}) %all-to-all-start.1) | async-done | bytes 393248 | tf_op jit(solution)/shard_map/all_to_all | solution.py:127
  152.8 0.4 reshape.318
  153.3 1.1 copy.113
  154.3 0.4 reshape.316
  154.8 0.5 copy.108
  155.3 1.6 fusion.20
  156.9 22.5 %while.39 = (s32[]{:T(128)}, f32[1,128,128]{2,1,0:T(8,128)S(1)}, bf16[24,1,128,64]{3,2,1,0:T(8,128)(2,1)}, bf16[24,1,128,64]{2,3,0,1:T(8,128)(2,1)S(1)}, f32[24,...) while((s32[]{:T(128)}, f32[1,128,128]{2,1,0:T(8,128)S(1)}, ...), condition=%wide.region_6.7_spmd.clone, body=%wide.region_5.6_spmd.clone.sunk | while | flops 2211843 | bytes 184931 | solution.py:60
  156.9 0.9 fusion.65
  157.9 0.9 fusion.65
  158.8 0.9 fusion.65
  159.7 0.9 fusion.65
  160.7 0.9 fusion.65
  161.6 0.9 fusion.65
  162.5 0.9 fusion.65
  163.5 0.9 fusion.65
  164.4 0.9 fusion.65
  165.4 0.9 fusion.65
  166.3 0.9 fusion.65
  167.2 0.9 fusion.65
  168.2 0.9 fusion.65
  169.1 0.9 fusion.65
  170.1 0.9 fusion.65
  171.0 0.9 fusion.65
  171.9 0.9 fusion.65
  172.9 0.9 fusion.65
  173.8 0.9 fusion.65
  174.7 0.9 fusion.65
  175.7 0.9 fusion.65
  176.6 0.9 fusion.65
  177.6 0.9 fusion.65
  178.5 0.9 fusion.65
  179.4 0.5 copy.111
  179.9 0.5 multiply_convert_fusion
  180.4 0.5 copy.118
  181.0 0.9 fusion.18
  182.1 1.6 fusion.34
  183.7 35.2 %all-gather.7.cloned.1.call-done = f32[96,64,128]{2,1,0:T(8,128)} async-done(((f32[24,64,128]{2,1,0:T(8,128)}), f32[96,64,128]{2,1,0:T(8,128)}) %all-gather.7.cloned.1.call-update) | async-done | bytes 3145744 | tf_op jit(solution)/shard_map/all_gather | solution.py:12
  219.0 4.2 %while.38 = (s32[]{:T(128)}, f32[1,24,64,128]{3,2,1,0:T(8,128)S(1)}, s32[]{:T(128)}, f32[4,1,24]{2,1,0:T(1,128)S(1)}, f32[4,1,24,64,128]{4,3,2,1,0:T(8,128)}, /*index=5*/s32[]{:T(128)}, s32[]{:T(128)}, s32[]{:T(128)}, s32[]{:T(128)}) while((s32[]{:T(128)}, f32[1,24,64,128]{3,2,1,0:T(8,128)S(1)}, s32[]{:T(128)}, f32[4,1,24]{2,1,0:T(1,128)S(1)}, ...), condition=%wide.region_4.5_spmd, body=%wide.region_3.4_spmd.sunk | while | flops 393222 | bytes 2359731 | solution.py:21
  219.0 1.4 bitcast_add_fusion.5
  220.4 1.3 bitcast_add_fusion.5
  221.8 1.3 bitcast_add_fusion.5
  223.2 0.7 fusion.14
  224.0 0.9 copy.119
  224.9 0.9 fusion.19
  (78 shorter events, 2.4 us)
Async XLA Ops:
  7.2 71.9 %all-gather.5.cloned.1.call-start = ((), (), s32[]{:S(2)}) async-start(), calls=%async_computation.2 | async-start | bytes 3932160 | tf_op jit(solution)/shard_map/all_gather | solution.py:12
  9.2 16.4 %copy-start.3 = (bf16[1,128,128]{2,1,0:T(8,128)(2,1)S(1)}, bf16[1,128,128]{2,1,0:T(8,128)(2,1)}, u32[]{:S(2)}) copy-start(bf16[1,128,128]{2,1,0:T(8,128)(2,1)} %param.16) | copy-start | bytes 98308
  9.2 16.4 %copy-start.2 = (bf16[1,128,128]{2,1,0:T(8,128)(2,1)S(1)}, bf16[1,128,128]{2,1,0:T(8,128)(2,1)}, u32[]{:S(2)}) copy-start(bf16[1,128,128]{2,1,0:T(8,128)(2,1)} %param.15) | copy-start | bytes 98308
  25.7 54.3 %copy-start.4 = (f32[128,128]{1,0:T(8,128)}, f32[128,128]{1,0:T(8,128)S(1)}, u32[]{:S(2)}) copy-start(f32[128,128]{1,0:T(8,128)S(1)} %fusion.43) | copy-start | bytes 196612
  79.2 0.8 copy-start.6
  79.2 0.8 copy-start.8
  82.1 7.8 %copy-start.7 = (f32[3,1536]{1,0:T(4,128)S(1)}, f32[3,1536]{1,0:T(4,128)}, u32[]{:S(2)}) copy-start(f32[3,1536]{1,0:T(4,128)} %param.20) | copy-start | bytes 55300
  86.1 12.0 %all-to-all-start = ((bf16[8,2,12288]{2,1,0:T(2,128)(2,1)}), bf16[8,2,12288]{2,1,0:T(2,128)(2,1)S(1)}, u32[]{:S(2)}, u32[]{:S(2)}) async-start(bf16[8,2,12288]{2,1,0:T(2,128)(2,1)} %reshape.339), calls=%async_computation | async-start | bytes 786432 | tf_op jit(solution)/shard_map/all_to_all | solution.py:121
  89.7 8.8 %copy-start = (bf16[8,16,1536]{2,1,0:T(8,128)(2,1)S(1)}, bf16[8,16,1536]{2,1,0:T(8,128)(2,1)}, u32[]{:S(2)}) copy-start(bf16[8,16,1536]{2,1,0:T(8,128)(2,1)} %param.21) | copy-start | bytes 1179652
  140.9 11.9 %all-to-all-start.1 = ((bf16[8,16,1536]{2,1,0:T(8,128)(2,1)}), bf16[8,16,1536]{2,1,0:T(8,128)(2,1)S(1)}, u32[]{:S(2)}, u32[]{:S(2)}) async-start(bf16[8,16,1536]{2,1,0:T(8,128)(2,1)} %get-tuple-element.338), calls=%async_computation.1 | async-start | bytes 786432 | tf_op jit(solution)/shard_map/all_to_all | solution.py:127
  144.5 74.4 %all-gather.7.cloned.1.call-start = ((), (), s32[]{:S(2)}) async-start(), calls=%async_computation.3 | async-start | bytes 3932160 | tf_op jit(solution)/shard_map/all_gather | solution.py:12
  180.4 1.8 copy-start.5
  219.0 4.3 %copy-start.1 = (f32[24,64,128]{2,1,0:T(8,128)S(1)}, f32[24,64,128]{2,1,0:T(8,128)}, u32[]{:S(2)}) copy-start(f32[24,64,128]{2,1,0:T(8,128)} %fusion.34) | copy-start | bytes 2359300
  219.0 4.3 %copy-start.9 = (f32[24]{0:T(128)S(1)}, f32[24]{0:T(128)}, u32[]{:S(2)}) copy-start(f32[24]{0:T(128)} %param.19) | copy-start | bytes 292
Sparse Core Ops, SparseCore 0:
  12.9 66.1 all-gather.4
  157.0 61.8 all-gather.6
where the time goes:
time: 235 us; the launch traced here: 233 us
  waiting for transfers between devices  104 us (44%)
  blocking collectives  53.5 us (23%)
  matrix products  30.7 us (13%)
  between operations  14.4 us (6%)
  other arithmetic  11.6 us (5%)
  local copies, waits for them, and re-layouts  9.91 us (4%)
  starting transfers between devices  7.49 us (3%)
    all_gather x2, waiting for transfers between devices, prefix(): gathered = jax.tree.map(lambda a: lax.all_gather(a, axis), part)  88.5 us
    psum x1, blocking collectives, per_device(): grad_kernel = lax.psum(kernel_part, ('gz', 'lat')) / math.sqrt(row_total)  40.9 us
    dot_general x24, matrix products, accumulate(): jnp.dot(grad_head, feat_head.T, preferred_element_type=jnp.float32)  21.5 us
    all_gather x1, blocking collectives, prefix(): gathered = jax.tree.map(lambda a: lax.all_gather(a, axis), part)  12.6 us
    all_to_all x1, waiting for transfers between devices, per_device(): lax.all_to_all(ssd_out, 'lat', split_axis=1, concat_axis=0, tiled=True)  8.08 us
    all_to_all x1, waiting for transfers between devices, per_device(): lax.all_to_all(grad_planes, 'lat', split_axis=0, concat_axis=1, tiled=True)  7.47 us
    unnamed x29, local copies, waits for them, and re-layouts  6.1 us
  transfers between devices with their start and end apart: 4, of which 4 were waited for; matrix products, arithmetic and copies ran while one was open for 12% of the time, Pallas kernels for 0%

commit v1 on v0

--- a/solution.py
+++ b/solution.py
@@ -126,7 +126,7 @@
     grad_planes = lateral_sum(jnp.pad(cotangent, widths), kernel, extent, True).astype(jnp.bfloat16)
     grad_ssd = lax.all_to_all(grad_planes, "lat", split_axis=0, concat_axis=1, tiled=True)
     kernel_part = kernel_terms(cotangent, padded_out, extent)
-    grad_kernel = lax.psum(kernel_part, ("gz", "lat")) / math.sqrt(row_total)
+    grad_kernel = jnp.sum(lax.all_gather(kernel_part, ("gz", "lat")), axis=0) / math.sqrt(row_total)
     heads_grad = grad_ssd.reshape(columns, sections, head_count, head_size)
     block_adjoint = jnp.einsum(
         "cjhn,cjhp->chpn", out_read, heads_grad, preferred_element_type=jnp.float32

time: 235 us -> 235 us (level)
  blocking collectives: 53.5 us -> 56.1 us
    all_gather x0 -> x1, blocking collectives: none -> 43.5 us  [per_device(): lax.all_gather(kernel_part, ('gz', 'lat'))]
    psum x1 -> x0, blocking collectives: 40.9 us -> none  [per_device(): grad_kernel = lax.psum(kernel_part, ('gz', 'lat')) / math.sqrt(row_total)]
where the time goes in v1:
time: 235 us; the launch traced here: 233 us
  waiting for transfers between devices  102 us (43%)
  blocking collectives  56.1 us (24%)
  matrix products  30.7 us (13%)
  between operations  14.4 us (6%)
  other arithmetic  11.7 us (5%)
  local copies, waits for them, and re-layouts  9.91 us (4%)
  starting transfers between devices  7.36 us (3%)
    all_gather x2, waiting for transfers between devices, prefix(): gathered = jax.tree.map(lambda a: lax.all_gather(a, axis), part)  86.5 us
    all_gather x1, blocking collectives, per_device(): lax.all_gather(kernel_part, ('gz', 'lat'))  43.5 us
    dot_general x24, matrix products, accumulate(): jnp.dot(grad_head, feat_head.T, preferred_element_type=jnp.float32)  21.5 us
    all_gather x1, blocking collectives, prefix(): gathered = jax.tree.map(lambda a: lax.all_gather(a, axis), part)  12.6 us
    all_to_all x1, waiting for transfers between devices, per_device(): lax.all_to_all(ssd_out, 'lat', split_axis=1, concat_axis=0, tiled=True)  8.08 us
    all_to_all x1, waiting for transfers between devices, per_device(): lax.all_to_all(grad_planes, 'lat', split_axis=0, concat_axis=1, tiled=True)  7.27 us
    unnamed x29, local copies, waits for them, and re-layouts  6.1 us
  transfers between devices with their start and end apart: 4, of which 4 were waited for; matrix products, arithmetic and copies ran while one was open for 12% of the time, Pallas kernels for 0%

profile of v1, /device:TPU:0, one launch (start us, length us, event | category | flops | bytes accessed | tf_op | source)
XLA Modules:
  0.0 233.0 jit_solution(17454946045736542749)
XLA Ops:
  7.2 0.8 copy.102
  8.0 0.8 negate_multiply_fusion
  9.2 1.2 copy.101
  10.4 0.8 bitcast_convert_fusion
  11.2 1.6 convolution_bitcast_fusion
  12.9 12.6 %all_gather.24 = f32[4,1,24]{2,1,0:T(1,128)S(1)} all-gather(f32[1,1,24]{2,1,0:T(1,128)S(1)} %get-tuple-element.337), channel_id=1, replica_groups=mesh['gz'=4,'lat'=8] {'gz'}, dimensions={0}, use_global_device_ids=true | all-gather | bytes 480 | tf_op jit(solution)/shard_map/all_gather | solution.py:12
  25.7 53.4 %all-gather.7.cloned.1.call-done = f32[96,64,128]{2,1,0:T(8,128)} async-done(((f32[24,64,128]{2,1,0:T(8,128)}), f32[96,64,128]{2,1,0:T(8,128)}) %all-gather.7.cloned.1.call-update) | async-done | bytes 3145744 | tf_op jit(solution)/shard_map/all_gather | solution.py:12
  79.3 0.7 fusion.21
  80.0 0.8 fusion.15
  80.8 0.7 copy.107
  81.5 0.5 broadcast.126
  82.1 3.0 %reduce.13 = bf16[128,1536]{1,0:T(8,128)(2,1)S(1)} reduce(bf16[128,1,1536]{2,1,0:T(2,128)(2,1)S(1)} %bitcast.169, bf16[]{:T(256)} %broadcast.126), dimensions={1}, to_apply=%bitcast.132.reduce_sub_computation | reduce | bytes 786434
  85.1 1.0 reshape.343
  86.1 3.7 %all-to-all-start = ((bf16[8,2,12288]{2,1,0:T(2,128)(2,1)}), bf16[8,2,12288]{2,1,0:T(2,128)(2,1)S(1)}, u32[]{:S(2)}, u32[]{:S(2)}) async-start(bf16[8,2,12288]{2,1,0:T(2,128)(2,1)} %reshape.343), calls=%async_computation | async-start | bytes 786432 | tf_op jit(solution)/shard_map/all_to_all | solution.py:121
  90.0 8.1 %all-to-all-done = bf16[8,2,12288]{2,1,0:T(2,128)(2,1)S(1)} async-done(((bf16[8,2,12288]{2,1,0:T(2,128)(2,1)}), bf16[8,2,12288]{2,1,0:T(2,128)(2,1)S(1)}, u32[]{:S(2)}, u32[]{:S(2)}) %all-to-all-start) | async-done | bytes 393248 | tf_op jit(solution)/shard_map/all_to_all | solution.py:121
  98.0 0.4 reshape.344
  98.9 43.5 %all-gather.3 = f32[32,3,1536]{2,1,0:T(4,128)S(1)} all-gather(f32[1,3,1536]{2,1,0:T(4,128)S(1)} %maximum_bitcast_fusion), channel_id=4, replica_groups=mesh['gz'=4,'lat'=8] {'gz','lat'}, dimensions={0}, use_global_device_ids=true | all-gather | bytes 608256 | tf_op jit(solution)/shard_map/all_gather | solution.py:129
  142.3 1.2 add_convert_fusion
  143.5 3.5 %all-to-all-start.1 = ((bf16[8,16,1536]{2,1,0:T(8,128)(2,1)}), bf16[8,16,1536]{2,1,0:T(8,128)(2,1)S(1)}, u32[]{:S(2)}, u32[]{:S(2)}) async-start(bf16[8,16,1536]{2,1,0:T(8,128)(2,1)} %get-tuple-element.338), calls=%async_computation.1 | async-start | bytes 786432 | tf_op jit(solution)/shard_map/all_to_all | solution.py:127
  147.3 0.6 broadcast_multiply_fusion
  148.0 7.3 %all-to-all-done.1 = bf16[8,16,1536]{2,1,0:T(8,128)(2,1)S(1)} async-done(((bf16[8,16,1536]{2,1,0:T(8,128)(2,1)}), bf16[8,16,1536]{2,1,0:T(8,128)(2,1)S(1)}, u32[]{:S(2)}, u32[]{:S(2)}) %all-to-all-start.1) | async-done | bytes 393248 | tf_op jit(solution)/shard_map/all_to_all | solution.py:127
  155.2 0.4 reshape.318
  155.7 1.1 copy.113
  156.7 0.4 reshape.316
  157.2 0.5 copy.108
  157.7 1.6 fusion.20
  159.3 22.5 %while.39 = (s32[]{:T(128)}, f32[1,128,128]{2,1,0:T(8,128)S(1)}, bf16[24,1,128,64]{3,2,1,0:T(8,128)(2,1)}, bf16[24,1,128,64]{2,3,0,1:T(8,128)(2,1)S(1)}, f32[24,...) while((s32[]{:T(128)}, f32[1,128,128]{2,1,0:T(8,128)S(1)}, ...), condition=%wide.region_6.7_spmd.clone, body=%wide.region_5.6_spmd.clone.sunk | while | flops 2211843 | bytes 184931 | solution.py:60
  159.3 0.9 fusion.65
  160.3 0.9 fusion.65
  161.2 0.9 fusion.65
  162.1 0.9 fusion.65
  163.1 0.9 fusion.65
  164.0 0.9 fusion.65
  165.0 0.9 fusion.65
  165.9 0.9 fusion.65
  166.8 0.9 fusion.65
  167.8 0.9 fusion.65
  168.7 0.9 fusion.65
  169.6 0.9 fusion.65
  170.6 0.9 fusion.65
  171.5 0.9 fusion.65
  172.5 0.9 fusion.65
  173.4 0.9 fusion.65
  174.3 0.9 fusion.65
  175.3 0.9 fusion.65
  176.2 0.9 fusion.65
  177.1 0.9 fusion.65
  178.1 0.9 fusion.65
  179.0 0.9 fusion.65
  180.0 0.9 fusion.65
  180.9 0.9 fusion.65
  181.8 0.5 copy.111
  182.3 0.5 multiply_convert_fusion
  182.8 0.5 copy.118
  183.4 0.9 fusion.18
  184.5 1.6 fusion.34
  186.1 33.1 %all-gather.9.cloned.1.call-done = f32[96,64,128]{2,1,0:T(8,128)} async-done(((f32[24,64,128]{2,1,0:T(8,128)}), f32[96,64,128]{2,1,0:T(8,128)}) %all-gather.9.cloned.1.call-update) | async-done | bytes 3145744 | tf_op jit(solution)/shard_map/all_gather | solution.py:12
  219.3 4.2 %while.38 = (s32[]{:T(128)}, f32[1,24,64,128]{3,2,1,0:T(8,128)S(1)}, s32[]{:T(128)}, f32[4,1,24]{2,1,0:T(1,128)S(1)}, f32[4,1,24,64,128]{4,3,2,1,0:T(8,128)}, /*index=5*/s32[]{:T(128)}, s32[]{:T(128)}, s32[]{:T(128)}, s32[]{:T(128)}) while((s32[]{:T(128)}, f32[1,24,64,128]{3,2,1,0:T(8,128)S(1)}, s32[]{:T(128)}, f32[4,1,24]{2,1,0:T(1,128)S(1)}, ...), condition=%wide.region_4.5_spmd, body=%wide.region_3.4_spmd.sunk | while | flops 393222 | bytes 2359731 | solution.py:21
  219.4 1.4 bitcast_add_fusion.5
  220.8 1.3 bitcast_add_fusion.5
  222.2 1.3 bitcast_add_fusion.5
  223.6 0.7 fusion.14
  224.3 0.9 copy.119
  225.3 0.9 fusion.19
  (79 shorter events, 2.5 us)
Async XLA Ops:
  7.2 71.9 %all-gather.7.cloned.1.call-start = ((), (), s32[]{:S(2)}) async-start(), calls=%async_computation.2 | async-start | bytes 3932160 | tf_op jit(solution)/shard_map/all_gather | solution.py:12
  9.2 16.4 %copy-start.3 = (bf16[1,128,128]{2,1,0:T(8,128)(2,1)S(1)}, bf16[1,128,128]{2,1,0:T(8,128)(2,1)}, u32[]{:S(2)}) copy-start(bf16[1,128,128]{2,1,0:T(8,128)(2,1)} %param.16) | copy-start | bytes 98308
  9.2 16.4 %copy-start.2 = (bf16[1,128,128]{2,1,0:T(8,128)(2,1)S(1)}, bf16[1,128,128]{2,1,0:T(8,128)(2,1)}, u32[]{:S(2)}) copy-start(bf16[1,128,128]{2,1,0:T(8,128)(2,1)} %param.15) | copy-start | bytes 98308
  25.7 54.3 %copy-start.4 = (f32[128,128]{1,0:T(8,128)}, f32[128,128]{1,0:T(8,128)S(1)}, u32[]{:S(2)}) copy-start(f32[128,128]{1,0:T(8,128)S(1)} %fusion.43) | copy-start | bytes 196612
  79.2 0.8 copy-start.6
  79.2 0.8 copy-start.8
  82.1 7.8 %copy-start.7 = (f32[3,1536]{1,0:T(4,128)S(1)}, f32[3,1536]{1,0:T(4,128)}, u32[]{:S(2)}) copy-start(f32[3,1536]{1,0:T(4,128)} %param.20) | copy-start | bytes 55300
  86.1 12.0 %all-to-all-start = ((bf16[8,2,12288]{2,1,0:T(2,128)(2,1)}), bf16[8,2,12288]{2,1,0:T(2,128)(2,1)S(1)}, u32[]{:S(2)}, u32[]{:S(2)}) async-start(bf16[8,2,12288]{2,1,0:T(2,128)(2,1)} %reshape.343), calls=%async_computation | async-start | bytes 786432 | tf_op jit(solution)/shard_map/all_to_all | solution.py:121
  89.7 8.8 %copy-start = (bf16[8,16,1536]{2,1,0:T(8,128)(2,1)S(1)}, bf16[8,16,1536]{2,1,0:T(8,128)(2,1)}, u32[]{:S(2)}) copy-start(bf16[8,16,1536]{2,1,0:T(8,128)(2,1)} %param.21) | copy-start | bytes 1179652
  143.5 11.7 %all-to-all-start.1 = ((bf16[8,16,1536]{2,1,0:T(8,128)(2,1)}), bf16[8,16,1536]{2,1,0:T(8,128)(2,1)S(1)}, u32[]{:S(2)}, u32[]{:S(2)}) async-start(bf16[8,16,1536]{2,1,0:T(8,128)(2,1)} %get-tuple-element.338), calls=%async_computation.1 | async-start | bytes 786432 | tf_op jit(solution)/shard_map/all_to_all | solution.py:127
  147.0 72.2 %all-gather.9.cloned.1.call-start = ((), (), s32[]{:S(2)}) async-start(), calls=%async_computation.3 | async-start | bytes 3932160 | tf_op jit(solution)/shard_map/all_gather | solution.py:12
  182.8 1.8 copy-start.5
  219.3 4.3 %copy-start.1 = (f32[24,64,128]{2,1,0:T(8,128)S(1)}, f32[24,64,128]{2,1,0:T(8,128)}, u32[]{:S(2)}) copy-start(f32[24,64,128]{2,1,0:T(8,128)} %fusion.34) | copy-start | bytes 2359300
  219.3 4.3 %copy-start.9 = (f32[24]{0:T(128)S(1)}, f32[24]{0:T(128)}, u32[]{:S(2)}) copy-start(f32[24]{0:T(128)} %param.19) | copy-start | bytes 292
Sparse Core Ops, SparseCore 0:
  12.9 66.1 all-gather.6
  159.4 59.7 all-gather.8
